TPU v7x, 32 devices: a whole 2x2x4 slice. The times are simulated.
32 devices in a mesh: fsdp: 4 (over y, x), ctx: 4 (over z), tp: 2 (over core).
Axes of the slice: x: 2, y: 2, z: 4, core: 2. Of those that a mesh axis runs over, the one named last changes fastest.
Arguments:
- image_input: bfloat16 [4, 2048, 768], P('fsdp', 'ctx'), may hold values from -6 to 6
- image_segments: int32 [4, 2048], P('fsdp'), may hold values from 0 to 5, never falling along the last dimension, each value on 1 to 1536 neighbouring positions
- image_cotangent: bfloat16 [4, 2048, 768], P('fsdp', 'ctx'), may hold values from -6 to 6
- image_gains: bfloat16 [2, 768], P(None, 'fsdp'), may hold values from 0.099609375 to 1.8984375
- image_shifts: bfloat16 [4, 768], P(None, 'fsdp'), may hold values from -3 to 3
- image_head_bias: bfloat16 [2, 2304], P('tp', 'fsdp'), may hold values from -3 to 3
- image_qkv_weight: bfloat16 [3, 768, 768], P(None, 'fsdp', 'tp'), may hold values from -0.21875 to 0.21875
- image_proj_weight: bfloat16 [768, 768], P('tp', 'fsdp'), may hold values from -0.875 to 0.875
- image_up_weight: bfloat16 [768, 3072], P('fsdp', 'tp'), may hold values from -0.21875 to 0.21875
- image_down_weight: bfloat16 [3072, 768], P('tp', 'fsdp'), may hold values from -0.109375 to 0.109375
- text_input: bfloat16 [4, 2048, 512], P('fsdp', 'ctx'), may hold values from -6 to 6
- text_segments: int32 [4, 2048], P('fsdp'), may hold values from 0 to 5, never falling along the last dimension, each value on 1 to 1536 neighbouring positions
- text_cotangent: bfloat16 [4, 2048, 512], P('fsdp', 'ctx'), may hold values from -6 to 6
- text_gains: bfloat16 [2, 512], P(None, 'fsdp'), may hold values from 0.099609375 to 1.8984375
- text_shifts: bfloat16 [4, 512], P(None, 'fsdp'), may hold values from -3 to 3
- text_head_bias: bfloat16 [2, 1536], P('tp', 'fsdp'), may hold values from -3 to 3
- text_qkv_weight: bfloat16 [3, 512, 512], P(None, 'fsdp', 'tp'), may hold values from -0.25 to 0.25
- text_proj_weight: bfloat16 [512, 512], P('tp', 'fsdp'), may hold values from -1 to 1
- text_up_weight: bfloat16 [512, 2048], P('fsdp', 'tp'), may hold values from -0.25 to 0.25
- text_down_weight: bfloat16 [2048, 512], P('tp', 'fsdp'), may hold values from -0.125 to 0.125
Outputs:
- image_output: bfloat16 [4, 2048, 768], P('fsdp', 'ctx')
- image_input_grad: float32 [4, 2048, 768], P('fsdp', 'ctx')
- image_gains_grad: float32 [2, 768], P(None, 'fsdp')
- image_shifts_grad: float32 [4, 768], P(None, 'fsdp')
- image_head_bias_grad: float32 [2, 2304], P('tp', 'fsdp')
- image_qkv_grad: float32 [3, 768, 768], P(None, 'fsdp', 'tp')
- image_proj_grad: float32 [768, 768], P('tp', 'fsdp')
- image_up_grad: float32 [768, 3072], P('fsdp', 'tp')
- image_down_grad: float32 [3072, 768], P('tp', 'fsdp')
- text_output: bfloat16 [4, 2048, 512], P('fsdp', 'ctx')
- text_input_grad: float32 [4, 2048, 512], P('fsdp', 'ctx')
- text_gains_grad: float32 [2, 512], P(None, 'fsdp')
- text_shifts_grad: float32 [4, 512], P(None, 'fsdp')
- text_head_bias_grad: float32 [2, 1536], P('tp', 'fsdp')
- text_qkv_grad: float32 [3, 512, 512], P(None, 'fsdp', 'tp')
- text_proj_grad: float32 [512, 512], P('tp', 'fsdp')
- text_up_grad: float32 [512, 2048], P('fsdp', 'tp')
- text_down_grad: float32 [2048, 512], P('tp', 'fsdp')
Inputs may be any that keep to these rules, and one draw needn't show every extreme that they name: `image_segments`: along each sequence segment numbers never fall; every document has 1 to 1536 tokens, and one has exactly that many. `text_segments`: along each sequence segment numbers never fall; every document has 1 to 1536 tokens, and one has exactly that many.
All inputs are finite; a program needn't handle non-finite values.
Results may differ from a plain program's by a relative error of at most 0.012.
Values may be sent and summed in bfloat16 or wider, within the bound.
A program may use at most 128 MiB of HBM per device.

v0:
```python
import jax
import jax.numpy as jnp
from jax import lax
from jax.sharding import PartitionSpec as P

HD = 64


def layer_stats(rows):
    row_mean = jnp.mean(rows, axis=-1, keepdims=True)
    centred = rows - row_mean
    inv_std = lax.rsqrt(jnp.mean(centred * centred, axis=-1, keepdims=True) + 1e-05)
    return (centred * inv_std, inv_std)


def norm_back(grad_normed_out, normed, inv_std, gain):
    scaled = grad_normed_out * gain
    return inv_std * (
        scaled
        - jnp.mean(scaled, axis=-1, keepdims=True)
        - normed * jnp.mean(scaled * normed, axis=-1, keepdims=True)
    )


def tensor_sum(partial_rows):
    return lax.psum(partial_rows, "tp")


def run_block(
    rows_in,
    seg_row,
    cotangent,
    gains,
    shifts,
    head_bias,
    qkv_weight,
    proj_weight,
    up_weight,
    down_weight,
    causal,
):
    gain_full, shift_full, bias_full, qkv_full, proj_full, up_full, down_full = (
        lax.all_gather(gains, "fsdp", axis=1, tiled=True),
        lax.all_gather(shifts, "fsdp", axis=1, tiled=True),
        lax.all_gather(head_bias, "fsdp", axis=1, tiled=True),
        lax.all_gather(qkv_weight, "fsdp", axis=1, tiled=True),
        lax.all_gather(proj_weight, "fsdp", axis=1, tiled=True),
        lax.all_gather(up_weight, "fsdp", axis=0, tiled=True),
        lax.all_gather(down_weight, "fsdp", axis=1, tiled=True),
    )
    gain_vals = gain_full.astype(jnp.float32)
    shift_vals = shift_full.astype(jnp.float32)
    bias_vals = bias_full[0].astype(jnp.float32)
    tp_width = qkv_full.shape[2]
    local_rows = rows_in.shape[1]
    seq_length = seg_row.shape[1]
    head_local = tp_width // HD
    rows = rows_in[0].astype(jnp.float32)
    row_start = lax.axis_index("ctx") * local_rows
    seg_all = seg_row[0]
    seg_query = lax.dynamic_slice_in_dim(seg_all, row_start, local_rows)
    query_pos = row_start + jnp.arange(local_rows, dtype=jnp.int32)
    key_pos = jnp.arange(seq_length, dtype=jnp.int32)
    allowed = seg_query[:, None] == seg_all[None, :]
    if causal:
        allowed = jnp.logical_and(allowed, key_pos[None, :] <= query_pos[:, None])

    def to_heads(matrix):
        return matrix.reshape(matrix.shape[0], head_local, HD).transpose(1, 0, 2)

    def from_heads(stacked):
        return stacked.transpose(1, 0, 2).reshape(stacked.shape[1], head_local * HD)

    normed_one, inv_one = layer_stats(rows)
    first_in = (normed_one * gain_vals[0] + shift_vals[0]).astype(jnp.bfloat16)
    queries = (
        jnp.dot(first_in, qkv_full[0], preferred_element_type=jnp.float32) + bias_vals[:tp_width]
    ).astype(jnp.bfloat16)
    key_rows = jnp.dot(first_in, qkv_full[1], preferred_element_type=jnp.float32).astype(
        jnp.bfloat16
    )
    values = (
        jnp.dot(first_in, qkv_full[2], preferred_element_type=jnp.float32)
        + bias_vals[tp_width : 2 * tp_width]
    ).astype(jnp.bfloat16)
    key_all, value_all = (
        lax.all_gather(key_rows, "ctx", axis=0, tiled=True),
        lax.all_gather(values, "ctx", axis=0, tiled=True),
    )
    query_heads = to_heads(queries)
    key_heads = to_heads(key_all)
    value_heads = to_heads(value_all)

    def attend(head_items):
        query_h, key_h, value_h = head_items
        scores = jnp.einsum("qd,kd->qk", query_h, key_h, preferred_element_type=jnp.float32) * 0.125
        scores = jnp.where(allowed, scores, -1e30)
        row_top = jnp.max(scores, axis=-1, keepdims=True)
        weights = jnp.exp(scores - row_top)
        row_total = jnp.sum(weights, axis=-1, keepdims=True)
        weights_low = (weights / row_total).astype(jnp.bfloat16)
        mixed_h = jnp.einsum("qk,kd->qd", weights_low, value_h, preferred_element_type=jnp.float32)
        return (mixed_h.astype(jnp.bfloat16), row_top[:, 0] + jnp.log(row_total[:, 0]))

    mixed_heads, log_totals = lax.map(attend, (query_heads, key_heads, value_heads))
    mixed = from_heads(mixed_heads)
    middle = (
        rows
        + tensor_sum(jnp.dot(mixed, proj_full, preferred_element_type=jnp.float32))
        + shift_vals[1]
    )
    normed_two, inv_two = layer_stats(middle)
    second_in = (normed_two * gain_vals[1] + shift_vals[2]).astype(jnp.bfloat16)
    hidden = (
        jnp.dot(second_in, up_full, preferred_element_type=jnp.float32) + bias_vals[2 * tp_width :]
    )
    sigma = jax.nn.sigmoid(1.702 * hidden)
    activated = (hidden * sigma).astype(jnp.bfloat16)
    output = (
        middle
        + tensor_sum(jnp.dot(activated, down_full, preferred_element_type=jnp.float32))
        + shift_vals[3]
    )
    grad_out = cotangent[0].astype(jnp.float32)
    grad_down_bias = jnp.sum(grad_out, axis=0)
    grad_branch = grad_out.astype(jnp.bfloat16)
    grad_down = jnp.einsum("tf,td->fd", activated, grad_branch, preferred_element_type=jnp.float32)
    grad_act = jnp.einsum("td,fd->tf", grad_branch, down_full, preferred_element_type=jnp.float32)
    grad_hidden = (grad_act * (sigma + 1.702 * hidden * sigma * (1.0 - sigma))).astype(jnp.bfloat16)
    grad_up_bias = jnp.sum(grad_hidden.astype(jnp.float32), axis=0)
    grad_up = jnp.einsum("td,tf->df", second_in, grad_hidden, preferred_element_type=jnp.float32)
    grad_second = tensor_sum(
        jnp.einsum("tf,df->td", grad_hidden, up_full, preferred_element_type=jnp.float32)
    )
    grad_gain_two = jnp.sum(grad_second * normed_two, axis=0)
    grad_shift_two = jnp.sum(grad_second, axis=0)
    grad_middle = grad_out + norm_back(grad_second, normed_two, inv_two, gain_vals[1])
    grad_proj_bias = jnp.sum(grad_middle, axis=0)
    grad_attn = grad_middle.astype(jnp.bfloat16)
    grad_proj = jnp.einsum("tc,td->cd", mixed, grad_attn, preferred_element_type=jnp.float32)
    grad_mixed = jnp.einsum(
        "td,cd->tc", grad_attn, proj_full, preferred_element_type=jnp.float32
    ).astype(jnp.bfloat16)

    def attend_back(head_items):
        query_h, key_h, value_h, grad_h, log_total = head_items
        scores = jnp.einsum("qd,kd->qk", query_h, key_h, preferred_element_type=jnp.float32) * 0.125
        weights = jnp.where(allowed, jnp.exp(scores - log_total[:, None]), 0.0)
        grad_weights = jnp.einsum("qd,kd->qk", grad_h, value_h, preferred_element_type=jnp.float32)
        row_delta = jnp.sum(weights * grad_weights, axis=-1, keepdims=True)
        grad_scores = (weights * (grad_weights - row_delta)).astype(jnp.bfloat16)
        grad_query_h = (
            jnp.einsum("qk,kd->qd", grad_scores, key_h, preferred_element_type=jnp.float32) * 0.125
        )
        grad_key_h = (
            jnp.einsum("qk,qd->kd", grad_scores, query_h, preferred_element_type=jnp.float32)
            * 0.125
        )
        grad_value_h = jnp.einsum(
            "qk,qd->kd", weights.astype(jnp.bfloat16), grad_h, preferred_element_type=jnp.float32
        )
        return (grad_query_h, grad_key_h, grad_value_h)

    query_parts, key_parts, value_parts = lax.map(
        attend_back, (query_heads, key_heads, value_heads, to_heads(grad_mixed), log_totals)
    )
    key_sum, value_sum = (
        lax.psum_scatter(from_heads(key_parts), "ctx", scatter_dimension=0, tiled=True),
        lax.psum_scatter(from_heads(value_parts), "ctx", scatter_dimension=0, tiled=True),
    )
    grad_query = from_heads(query_parts).astype(jnp.bfloat16)
    grad_key = key_sum.astype(jnp.bfloat16)
    grad_value = value_sum.astype(jnp.bfloat16)
    grad_qkv = jnp.stack(
        [
            jnp.einsum("td,tc->dc", first_in, grad_query, preferred_element_type=jnp.float32),
            jnp.einsum("td,tc->dc", first_in, grad_key, preferred_element_type=jnp.float32),
            jnp.einsum("td,tc->dc", first_in, grad_value, preferred_element_type=jnp.float32),
        ]
    )
    grad_head = jnp.concatenate(
        [
            jnp.sum(grad_query.astype(jnp.float32), axis=0),
            jnp.sum(grad_value.astype(jnp.float32), axis=0),
            grad_up_bias,
        ]
    )[None, :]
    grad_first_part = jnp.einsum(
        "tc,dc->td", grad_query, qkv_full[0], preferred_element_type=jnp.float32
    )
    grad_first_part = grad_first_part + jnp.einsum(
        "tc,dc->td", grad_key, qkv_full[1], preferred_element_type=jnp.float32
    )
    grad_first_part = grad_first_part + jnp.einsum(
        "tc,dc->td", grad_value, qkv_full[2], preferred_element_type=jnp.float32
    )
    grad_first = tensor_sum(grad_first_part)
    grad_gain_one = jnp.sum(grad_first * normed_one, axis=0)
    grad_shift_one = jnp.sum(grad_first, axis=0)
    grad_rows = grad_middle + norm_back(grad_first, normed_one, inv_one, gain_vals[0])
    grad_gains = jnp.stack([grad_gain_one, grad_gain_two])
    grad_shifts = jnp.stack([grad_shift_one, grad_proj_bias, grad_shift_two, grad_down_bias])
    share_gains, share_shifts, share_head, share_qkv, share_proj, share_up, share_down = (
        lax.psum_scatter(grad_gains, "fsdp", scatter_dimension=1, tiled=True),
        lax.psum_scatter(grad_shifts, "fsdp", scatter_dimension=1, tiled=True),
        lax.psum_scatter(grad_head, "fsdp", scatter_dimension=1, tiled=True),
        lax.psum_scatter(grad_qkv, "fsdp", scatter_dimension=1, tiled=True),
        lax.psum_scatter(grad_proj, "fsdp", scatter_dimension=1, tiled=True),
        lax.psum_scatter(grad_up, "fsdp", scatter_dimension=0, tiled=True),
        lax.psum_scatter(grad_down, "fsdp", scatter_dimension=1, tiled=True),
    )
    owned = lax.psum(
        (share_gains, share_shifts, share_head, share_qkv, share_proj, share_up, share_down), "ctx"
    )
    return (output.astype(jnp.bfloat16)[None], grad_rows[None]) + tuple(owned)


def on_device(
    image_input,
    image_segments,
    image_cotangent,
    image_gains,
    image_shifts,
    image_head_bias,
    image_qkv_weight,
    image_proj_weight,
    image_up_weight,
    image_down_weight,
    text_input,
    text_segments,
    text_cotangent,
    text_gains,
    text_shifts,
    text_head_bias,
    text_qkv_weight,
    text_proj_weight,
    text_up_weight,
    text_down_weight,
):
    image_results = run_block(
        image_input,
        image_segments,
        image_cotangent,
        image_gains,
        image_shifts,
        image_head_bias,
        image_qkv_weight,
        image_proj_weight,
        image_up_weight,
        image_down_weight,
        False,
    )
    text_results = run_block(
        text_input,
        text_segments,
        text_cotangent,
        text_gains,
        text_shifts,
        text_head_bias,
        text_qkv_weight,
        text_proj_weight,
        text_up_weight,
        text_down_weight,
        True,
    )
    return image_results + text_results


def solution(mesh):
    return jax.shard_map(
        on_device,
        mesh=mesh,
        in_specs=(
            P("fsdp", "ctx", None),
            P("fsdp", None),
            P("fsdp", "ctx", None),
            P(None, "fsdp"),
            P(None, "fsdp"),
            P("tp", "fsdp"),
            P(None, "fsdp", "tp"),
            P("tp", "fsdp"),
            P("fsdp", "tp"),
            P("tp", "fsdp"),
            P("fsdp", "ctx", None),
            P("fsdp", None),
            P("fsdp", "ctx", None),
            P(None, "fsdp"),
            P(None, "fsdp"),
            P("tp", "fsdp"),
            P(None, "fsdp", "tp"),
            P("tp", "fsdp"),
            P("fsdp", "tp"),
            P("tp", "fsdp"),
        ),
        out_specs=(
            P("fsdp", "ctx", None),
            P("fsdp", "ctx", None),
            P(None, "fsdp"),
            P(None, "fsdp"),
            P("tp", "fsdp"),
            P(None, "fsdp", "tp"),
            P("tp", "fsdp"),
            P("fsdp", "tp"),
            P("tp", "fsdp"),
            P("fsdp", "ctx", None),
            P("fsdp", "ctx", None),
            P(None, "fsdp"),
            P(None, "fsdp"),
            P("tp", "fsdp"),
            P(None, "fsdp", "tp"),
            P("tp", "fsdp"),
            P("fsdp", "tp"),
            P("tp", "fsdp"),
        ),
        check_vma=False,
    )
```

profile of v0, /device:TPU:0, one launch (start us, length us, event | category | flops | bytes accessed | tf_op | source)
XLA Modules:
  0.0 1437.0 jit_solution(6078367909397916896)
XLA Ops:
  8.0 9.5 all_gather.63
  17.5 7.9 all_gather.66
  25.4 7.2 all_gather.64
  33.9 16.2 %all_gather.65 = bf16[3,512,256]{2,1,0:T(8,128)(2,1)S(1)} all-gather(bf16[3,128,256]{2,1,0:T(8,128)(2,1)} %param.44), channel_id=1, replica_groups=mesh['fsdp'=4,'ctx'=4,'tp'=2] {'fsdp'}, dimensions={1}, use_global_device_ids=true | all-gather | bytes 983040 | tf_op jit(solution)/shard_map/all_gather | solution.py:46
  53.6 7.6 all-gather.1
  61.4 7.5 all-gather
  70.5 9.3 all-reduce
  85.0 8.5 all_gather.69
  93.6 9.8 all_gather.60
  116.6 30.7 %while.58 = (s32[]{:T(128)}, bf16[4,512,64]{1,2,0:T(8,128)(2,1)S(1)}, f32[4,512]{1,0:T(4,128)S(1)}, bf16[4,512,64]{2,1,0:T(8,128)(2,1)}, bf16[4,2048,64]{2,1,0:T...) while((s32[]{:T(128)}, ...), condition=%wide.region_49.50_spmd.clone, body=%wide.region_46.49_spmd.clone.sunk | while | flops 280002048 | bytes 30640268 | solution.py:105
  153.4 4.2 copy.88
  157.6 29.2 %all-gather.14.cloned.1.call-done = bf16[2048,384]{1,0:T(8,128)(2,1)} async-done(((bf16[512,384]{1,0:T(8,128)(2,1)}), bf16[2048,384]{1,0:T(8,128)(2,1)}) %all-gather.14.cloned.1.call-update) | async-done | bytes 1572880 | tf_op jit(solution)/shard_map/all_gather | solution.py:87
  189.4 4.2 copy.87
  193.5 43.0 %while.56 = (s32[]{:T(128)}, bf16[6,512,64]{1,2,0:T(8,128)(2,1)S(1)}, f32[6,512]{1,0:T(8,128)S(1)}, bf16[6,512,64]{2,1,0:T(8,128)(2,1)S(1)}, bf16[6,2048,64]{2,1...) while((s32[]{:T(128)}, ...), condition=%wide.region_5.6_spmd.clone, body=%wide.region_2.5_spmd.clone.sunk | while | flops 277904896 | bytes 30638212 | solution.py:105
  241.5 18.1 %all-reduce.17.cloned.1.call-done = (f32[512,768]{1,0:T(8,128)}, f32[512,512]{1,0:T(8,128)}) async-done(((f32[512,768]{1,0:T(8,128)}, f32[512,512]{1,0:T(8,128)}), (f32[512,768]{1,0:T(8,128)}, f32[512,512]{1,0:T(8,128)})) %all-reduce.17.cloned.1.call-update) | async-done | bytes 2621456 | tf_op jit(solution)/shard_map/psum | solution.py:26
  262.1 27.4 %all-gather.26.cloned.1.call-done = bf16[512,1024]{1,0:T(8,128)(2,1)} async-done(((bf16[128,1024]{1,0:T(8,128)(2,1)}), bf16[512,1024]{1,0:T(8,128)(2,1)}) %all-gather.26.cloned.1.call-update) | async-done | bytes 1048592 | tf_op jit(solution)/shard_map/all_gather | solution.py:48
  289.5 3.9 multiply_convert_fusion.4
  293.4 24.6 %all-gather.28.cloned.1.call-done = bf16[1024,512]{1,0:T(8,128)(2,1)} async-done(((bf16[1024,128]{1,0:T(8,128)(2,1)}), bf16[1024,512]{1,0:T(8,128)(2,1)}) %all-gather.28.cloned.1.call-update) | async-done | bytes 1048592 | tf_op jit(solution)/shard_map/all_gather | solution.py:49
  318.0 3.8 convert_reduce_fusion.2
  324.5 33.0 %all-gather.18.cloned.1.call-done = bf16[768,1536]{1,0:T(8,128)(2,1)} async-done(((bf16[192,1536]{1,0:T(8,128)(2,1)}), bf16[768,1536]{1,0:T(8,128)(2,1)}) %all-gather.18.cloned.1.call-update) | async-done | bytes 2359312 | tf_op jit(solution)/shard_map/all_gather | solution.py:48
  357.5 4.8 convolution_add_fusion
  362.3 34.5 %all-gather.20.cloned.1.call-done = bf16[1536,768]{0,1:T(8,128)(2,1)} async-done(((bf16[1536,192]{0,1:T(8,128)(2,1)}), bf16[1536,768]{0,1:T(8,128)(2,1)}) %all-gather.20.cloned.1.call-update) | async-done | bytes 2359312 | tf_op jit(solution)/shard_map/all_gather | solution.py:49
  396.8 5.6 convert_reduce_fusion
  406.5 22.1 %all-reduce.15.cloned.1.call-done = (f32[512,768]{1,0:T(8,128)}, f32[512,512]{1,0:T(8,128)}) async-done(((f32[512,768]{1,0:T(8,128)}, f32[512,512]{1,0:T(8,128)}), (f32[512,768]{1,0:T(8,128)}, f32[512,512]{1,0:T(8,128)})) %all-reduce.15.cloned.1.call-update) | async-done | bytes 2621456 | tf_op jit(solution)/shard_map/psum | solution.py:26
  435.3 31.2 %while.59 = (s32[]{:T(128)}, bf16[4,512,64]{1,2,0:T(8,128)(2,1)S(1)}, f32[4,2048,64]{1,2,0:T(8,128)}, f32[4,2048,64]{1,2,0:T(8,128)}, bf16[4,512,64]{2,1,0:T(8,1...) while((s32[]{:T(128)}, ...), condition=%wide.region_59.60_spmd.clone, body=%wide.region_57.59_spmd.clone.sunk | while | flops 683834880 | bytes 40004792 | solution.py:164
  474.8 65.2 %while.57 = (s32[]{:T(128)}, bf16[6,512,64]{1,2,0:T(8,128)(2,1)}, f32[6,2048,64]{1,2,0:T(8,128)}, f32[6,2048,64]{1,2,0:T(8,128)}, bf16[6,512,64]{2,1,0:T(8,128)(...) while((s32[]{:T(128)}, bf16[6,512,64]{1,2,0:T(8,128)(2,1)}, ...), condition=%wide.region_15.16_spmd.clone, body=%wide.region_13.15_spmd.clone.sunk | while | flops 681737728 | bytes 34759800 | solution.py:164
  544.5 4.9 fusion.171
  560.1 59.0 %reduce-scatter.31.cloned.1.call-done = f32[512,384]{0,1:T(8,128)} async-done(((f32[2048,384]{0,1:T(8,128)}), f32[512,384]{0,1:T(8,128)}) %reduce-scatter.31.cloned.1.call-update) | async-done | bytes 786448 | tf_op jit(solution)/shard_map/reduce_scatter | solution.py:168
  622.2 59.4 %reduce-scatter.33.cloned.1.call-done = f32[512,384]{0,1:T(8,128)} async-done(((f32[2048,384]{0,1:T(8,128)}), f32[512,384]{0,1:T(8,128)}) %reduce-scatter.33.cloned.1.call-update) | async-done | bytes 786448 | tf_op jit(solution)/shard_map/reduce_scatter | solution.py:169
  681.6 4.1 add_add_fusion
  700.3 5.1 fusion.170
  706.7 6.2 fusion.139
  739.8 5.9 reduce-scatter.49.cloned.1.call-done
  745.7 38.0 %reduce-scatter.51.cloned.1.call-done = f32[128,1024]{1,0:T(8,128)} async-done(((f32[512,1024]{1,0:T(8,128)}), f32[128,1024]{1,0:T(8,128)}) %reduce-scatter.51.cloned.1.call-update) | async-done | bytes 524304 | tf_op jit(solution)/shard_map/reduce_scatter | solution.py:209
  783.7 38.4 %reduce-scatter.53.cloned.1.call-done = f32[1024,128]{1,0:T(8,128)} async-done(((f32[1024,512]{1,0:T(8,128)}), f32[1024,128]{1,0:T(8,128)}) %reduce-scatter.53.cloned.1.call-update) | async-done | bytes 524304 | tf_op jit(solution)/shard_map/reduce_scatter | solution.py:210
  822.1 31.9 %reduce-scatter.37.cloned.1.call-done = f32[384,192]{0,1:T(8,128)} async-done(((f32[384,768]{0,1:T(8,128)}), f32[384,192]{0,1:T(8,128)}) %reduce-scatter.37.cloned.1.call-update) | async-done | bytes 294928 | tf_op jit(solution)/shard_map/reduce_scatter | solution.py:208
  854.1 60.1 %reduce-scatter.39.cloned.1.call-done = f32[192,1536]{1,0:T(8,128)} async-done(((f32[768,1536]{1,0:T(8,128)}), f32[192,1536]{1,0:T(8,128)}) %reduce-scatter.39.cloned.1.call-update) | async-done | bytes 1179664 | tf_op jit(solution)/shard_map/reduce_scatter | solution.py:209
  914.2 60.1 %reduce-scatter.41.cloned.1.call-done = f32[1536,192]{0,1:T(8,128)} async-done(((f32[1536,768]{0,1:T(8,128)}), f32[1536,192]{0,1:T(8,128)}) %reduce-scatter.41.cloned.1.call-update) | async-done | bytes 1179664 | tf_op jit(solution)/shard_map/reduce_scatter | solution.py:210
  974.3 34.0 %reduce-scatter.47.cloned.1.call-done = f32[3,128,256]{2,1,0:T(8,128)} async-done(((f32[3,512,256]{2,1,0:T(8,128)}), f32[3,128,256]{2,1,0:T(8,128)}) %reduce-scatter.47.cloned.1.call-update) | async-done | bytes 393232 | tf_op jit(solution)/shard_map/reduce_scatter | solution.py:207
  1008.3 50.2 %reduce-scatter.35.cloned.1.call-done = f32[3,192,384]{2,1,0:T(8,128)} async-done(((f32[3,768,384]{2,1,0:T(8,128)}), f32[3,192,384]{2,1,0:T(8,128)}) %reduce-scatter.35.cloned.1.call-update) | async-done | bytes 884752 | tf_op jit(solution)/shard_map/reduce_scatter | solution.py:207
  1058.5 29.6 %reduce-scatter.65.cloned.1.call-done = f32[384,1]{1,0:T(8,128)} async-done(((f32[1536,1]{1,0:T(8,128)}), f32[384,1]{1,0:T(8,128)}) %reduce-scatter.65.cloned.1.call-update) | async-done | bytes 1552
  1089.1 30.9 %reduce-scatter.59.cloned.1.call-done = f32[576,1]{1,0:T(8,128)} async-done(((f32[2304,1]{1,0:T(8,128)}), f32[576,1]{1,0:T(8,128)}) %reduce-scatter.59.cloned.1.call-update) | async-done | bytes 2320
  1128.9 18.4 %reduce-scatter.61.cloned.1.call-done = f32[128,2]{1,0:T(8,128)} async-done(((f32[512,2]{1,0:T(8,128)}), f32[128,2]{1,0:T(8,128)}) %reduce-scatter.61.cloned.1.call-update) | async-done | bytes 1040
  1148.2 27.1 %reduce-scatter.55.cloned.1.call-done = f32[192,2]{1,0:T(8,128)} async-done(((f32[768,2]{1,0:T(8,128)}), f32[192,2]{1,0:T(8,128)}) %reduce-scatter.55.cloned.1.call-update) | async-done | bytes 1552
  1176.3 26.7 %reduce-scatter.63.cloned.1.call-done = f32[128,4]{1,0:T(8,128)} async-done(((f32[512,4]{1,0:T(8,128)}), f32[128,4]{1,0:T(8,128)}) %reduce-scatter.63.cloned.1.call-update) | async-done | bytes 2064
  1203.9 26.8 %reduce-scatter.57.cloned.1.call-done = f32[192,4]{1,0:T(8,128)} async-done(((f32[768,4]{1,0:T(8,128)}), f32[192,4]{1,0:T(8,128)}) %reduce-scatter.57.cloned.1.call-update) | async-done | bytes 3088
  1231.6 21.5 %all-reduce.1 = (f32[2,192]{1,0:T(2,128)}, f32[4,192]{1,0:T(4,128)}, f32[1,576]{1,0:T(1,128)}, f32[2,128]{1,0:T(2,128)}, f32[4,128]{1,0:T(4,128)}, /*index=5*/f32[1,384]{1,0:T(1,128)}) all-reduce(f32[2,192]{1,0:T(2,128)S(1)} %copy.101, f32[4,192]{1,0:T(4,128)S(1)} %copy.103, ...), channel_id=1, replica_groups=mesh['fsdp'=4,'ctx'=4,'tp'=2] {'ctx'}, use_global_device_ids=true, to_apply=%region_24.25 | all-reduce | flops 2880 | bytes 23040 | tf_op jit(solution)/shard_map/psum | solution.py:212
  1253.1 167.8 %all-reduce.11.cloned.1.call-done = (f32[3,192,384]{2,1,0:T(8,128)}, f32[384,192]{0,1:T(8,128)}, f32[192,1536]{1,0:T(8,128)}, f32[1536,192]{0,1:T(8,128)}, f32[3...) async-done(((f32[3,192,384]{2,1,0:T(8,128)}, f32[384,192]{0,1:T(8,128)}, f32[192,1536]{1,0:T(8,128)}, f32[1536,192]{0,1:T(8,128)}, ...) | async-done | bytes 5111824 | tf_op jit(solution)/shard_map/psum | solution.py:212
  (542 shorter events, 314.7 us)
Async XLA Ops:
  7.2 42.9 %copy-start.6 = (bf16[1,512,512]{2,1,0:T(8,128)(2,1)S(1)}, bf16[1,512,512]{2,1,0:T(8,128)(2,1)}, u32[]{:S(2)}) copy-start(bf16[1,512,512]{2,1,0:T(8,128)(2,1)} %param.38) | copy-start | bytes 1572868
  7.2 73.8 %all-gather.12.cloned.1.call-start = ((), (), s32[]{:S(2)}) async-start(), calls=%async_computation.18 | async-start | bytes 2211840 | tf_op jit(solution)/shard_map/all_gather | solution.py:46
  7.9 95.5 %all-gather.24.cloned.1.call-start = ((), (), s32[]{:S(2)}) async-start(), calls=%async_computation.30 | async-start | bytes 1310720 | tf_op jit(solution)/shard_map/all_gather | solution.py:88
  50.1 33.6 %copy-start.21 = (bf16[3,512,256]{2,1,0:T(8,128)(2,1)}, bf16[3,512,256]{2,1,0:T(8,128)(2,1)S(1)}, u32[]{:S(2)}) copy-start(bf16[3,512,256]{2,1,0:T(8,128)(2,1)S(1)} %all_gather.65) | copy-start | bytes 2359300
  50.5 18.5 %copy-start.90 = (u32[32]{0:T(128)S(1)}, u32[32]{0:T(128)}, u32[]{:S(2)}) copy-start(u32[32]{0:T(128)} %constant.151) | copy-start | bytes 388
  50.5 19.7 %copy-start.83 = (bf16[1,576]{1,0:T(2,128)(2,1)S(1)}, bf16[1,576]{1,0:T(2,128)(2,1)}, u32[]{:S(2)}) copy-start(bf16[1,576]{1,0:T(2,128)(2,1)} %param.33) | copy-start | bytes 3460
  50.5 29.9 %copy-start.4 = (bf16[1,512,768]{2,1,0:T(8,128)(2,1)S(1)}, bf16[1,512,768]{2,1,0:T(8,128)(2,1)}, u32[]{:S(2)}) copy-start(bf16[1,512,768]{2,1,0:T(8,128)(2,1)} %param.28) | copy-start | bytes 2359300
  51.4 32.3 %copy-start.31 = (bf16[512,512]{1,0:T(8,128)(2,1)}, bf16[512,512]{1,0:T(8,128)(2,1)S(1)}, u32[]{:S(2)}) copy-start(bf16[512,512]{1,0:T(8,128)(2,1)S(1)} %fusion.143) | copy-start | bytes 1572868
  52.4 57.8 %all-gather.22.cloned.1.call-start = ((), (), s32[]{:S(2)}) async-start(), calls=%async_computation.29 | async-start | bytes 1310720 | tf_op jit(solution)/shard_map/all_gather | solution.py:87
  53.5 97.3 %all-gather.16.cloned.1.call-start = ((), (), s32[]{:S(2)}) async-start(), calls=%async_computation.20 | async-start | bytes 1966080 | tf_op jit(solution)/shard_map/all_gather | solution.py:88
  79.8 68.8 %copy-start.56 = (f32[768]{0:T(1024)}, f32[768]{0:T(1024)S(1)}, u32[]{:S(2)}) copy-start(f32[768]{0:T(1024)S(1)} %get-tuple-element.453) | copy-start | bytes 9220
  80.4 68.2 %copy-start.78 = (f32[768]{0:T(1024)}, f32[768]{0:T(1024)S(1)}, u32[]{:S(2)}) copy-start(f32[768]{0:T(1024)S(1)} %get-tuple-element.449) | copy-start | bytes 9220
  80.4 277.1 %copy-start.80 = (f32[768]{0:T(1024)}, f32[768]{0:T(1024)S(1)}, u32[]{:S(2)}) copy-start(f32[768]{0:T(1024)S(1)} %get-tuple-element.447) | copy-start | bytes 9220
  80.6 68.0 %copy-start.62 = (f32[512]{0:T(512)}, f32[512]{0:T(512)S(1)}, u32[]{:S(2)}) copy-start(f32[512]{0:T(512)S(1)} %broadcast_multiply_fusion.11) | copy-start | bytes 6148
  81.0 67.7 %copy-start.64 = (f32[512]{0:T(512)}, f32[512]{0:T(512)S(1)}, u32[]{:S(2)}) copy-start(f32[512]{0:T(512)S(1)} %add_rsqrt_fusion.3) | copy-start | bytes 6148
  83.5 19.8 %copy-start.50 = (s32[1,2048]{1,0:T(1,128)S(1)}, s32[1,2048]{1,0:T(1,128)}, u32[]{:S(2)}) copy-start(s32[1,2048]{1,0:T(1,128)} %param.29) | copy-start | bytes 24580
  83.5 19.9 %copy-start.86 = (s32[1,2048]{1,0:T(1,128)S(1)}, s32[1,2048]{1,0:T(1,128)}, u32[]{:S(2)}) copy-start(s32[1,2048]{1,0:T(1,128)} %param.39) | copy-start | bytes 24580
  83.6 103.2 %all-gather.14.cloned.1.call-start = ((), (), s32[]{:S(2)}) async-start(), calls=%async_computation.19 | async-start | bytes 1966080 | tf_op jit(solution)/shard_map/all_gather | solution.py:87
  93.5 53.8 %copy-start.27 = (bf16[256,512]{1,0:T(8,128)(2,1)}, bf16[256,512]{1,0:T(8,128)(2,1)S(1)}, u32[]{:S(2)}) copy-start(bf16[256,512]{1,0:T(8,128)(2,1)S(1)} %all_gather.69) | copy-start | bytes 786436
  103.4 133.3 %copy-start.16 = (bf16[384,768]{0,1:T(8,128)(2,1)}, bf16[384,768]{0,1:T(8,128)(2,1)S(1)}, u32[]{:S(2)}) copy-start(bf16[384,768]{0,1:T(8,128)(2,1)S(1)} %all_gather.60) | copy-start | bytes 1769476
  116.0 143.6 %all-reduce.17.cloned.1.call-start = ((), (), s32[]{:S(2)}) async-start(), calls=%async_computation.48 | async-start | bytes 5242880 | tf_op jit(solution)/shard_map/psum | solution.py:26
  238.4 51.1 %all-gather.26.cloned.1.call-start = ((), (), s32[]{:S(2)}) async-start(), calls=%async_computation.31 | async-start | bytes 1310720 | tf_op jit(solution)/shard_map/all_gather | solution.py:48
  239.2 78.8 %all-gather.28.cloned.1.call-start = ((), (), s32[]{:S(2)}) async-start(), calls=%async_computation.32 | async-start | bytes 1310720 | tf_op jit(solution)/shard_map/all_gather | solution.py:49
  239.9 117.6 %all-gather.18.cloned.1.call-start = ((), (), s32[]{:S(2)}) async-start(), calls=%async_computation.21 | async-start | bytes 2949120 | tf_op jit(solution)/shard_map/all_gather | solution.py:48
  240.7 156.2 %all-gather.20.cloned.1.call-start = ((), (), s32[]{:S(2)}) async-start(), calls=%async_computation.22 | async-start | bytes 2949120 | tf_op jit(solution)/shard_map/all_gather | solution.py:49
  241.3 187.3 %all-reduce.15.cloned.1.call-start = ((), (), s32[]{:S(2)}) async-start(), calls=%async_computation.47 | async-start | bytes 5242880 | tf_op jit(solution)/shard_map/psum | solution.py:26
  289.5 28.5 %copy-start.29 = (bf16[1,512,512]{2,1,0:T(8,128)(2,1)S(1)}, bf16[1,512,512]{2,1,0:T(8,128)(2,1)}, u32[]{:S(2)}) copy-start(bf16[1,512,512]{2,1,0:T(8,128)(2,1)} %param.40) | copy-start | bytes 1572868
  406.2 147.4 %reduce-scatter.43.cloned.1.call-start = ((), (), s32[]{:S(2)}) async-start(), calls=%async_computation.33 | async-start | bytes 2621440 | tf_op jit(solution)/shard_map/reduce_scatter | solution.py:168
  466.5 90.8 %reduce-scatter.45.cloned.1.call-start = ((), (), s32[]{:S(2)}) async-start(), calls=%async_computation.34 | async-start | bytes 2621440 | tf_op jit(solution)/shard_map/reduce_scatter | solution.py:169
  474.8 144.3 %reduce-scatter.31.cloned.1.call-start = ((), (), s32[]{:S(2)}) async-start(), calls=%async_computation.23 | async-start | bytes 3932160 | tf_op jit(solution)/shard_map/reduce_scatter | solution.py:168
  540.0 141.6 %reduce-scatter.33.cloned.1.call-start = ((), (), s32[]{:S(2)}) async-start(), calls=%async_computation.24 | async-start | bytes 3932160 | tf_op jit(solution)/shard_map/reduce_scatter | solution.py:169
  540.6 192.2 %all-reduce.13.cloned.1.call-start = ((), (), s32[]{:S(2)}) async-start(), calls=%async_computation.46 | async-start | bytes 10485760 | tf_op jit(solution)/shard_map/psum | solution.py:26
  685.7 60.0 %reduce-scatter.49.cloned.1.call-start = ((), (), s32[]{:S(2)}) async-start(), calls=%async_computation.36 | async-start | bytes 655360 | tf_op jit(solution)/shard_map/reduce_scatter | solution.py:208
  688.9 94.8 %reduce-scatter.51.cloned.1.call-start = ((), (), s32[]{:S(2)}) async-start(), calls=%async_computation.37 | async-start | bytes 2621440 | tf_op jit(solution)/shard_map/reduce_scatter | solution.py:209
  692.5 129.7 %reduce-scatter.53.cloned.1.call-start = ((), (), s32[]{:S(2)}) async-start(), calls=%async_computation.38 | async-start | bytes 2621440 | tf_op jit(solution)/shard_map/reduce_scatter | solution.py:210
  697.1 157.0 %reduce-scatter.37.cloned.1.call-start = ((), (), s32[]{:S(2)}) async-start(), calls=%async_computation.26 | async-start | bytes 1474560 | tf_op jit(solution)/shard_map/reduce_scatter | solution.py:208
  700.3 213.9 %reduce-scatter.39.cloned.1.call-start = ((), (), s32[]{:S(2)}) async-start(), calls=%async_computation.27 | async-start | bytes 5898240 | tf_op jit(solution)/shard_map/reduce_scatter | solution.py:209
  705.5 268.8 %reduce-scatter.41.cloned.1.call-start = ((), (), s32[]{:S(2)}) async-start(), calls=%async_computation.28 | async-start | bytes 5898240 | tf_op jit(solution)/shard_map/reduce_scatter | solution.py:210
  712.9 295.3 %reduce-scatter.47.cloned.1.call-start = ((), (), s32[]{:S(2)}) async-start(), calls=%async_computation.35 | async-start | bytes 1966080 | tf_op jit(solution)/shard_map/reduce_scatter | solution.py:207
  718.9 339.6 %reduce-scatter.35.cloned.1.call-start = ((), (), s32[]{:S(2)}) async-start(), calls=%async_computation.25 | async-start | bytes 4423680 | tf_op jit(solution)/shard_map/reduce_scatter | solution.py:207
  725.1 362.9 %reduce-scatter.65.cloned.1.call-start = ((), (), s32[]{:S(2)}) async-start(), calls=%async_computation.44 | async-start | bytes 983040
  730.0 390.0 %reduce-scatter.59.cloned.1.call-start = ((), (), s32[]{:S(2)}) async-start(), calls=%async_computation.41 | async-start | bytes 1474560
  732.7 414.5 %reduce-scatter.61.cloned.1.call-start = ((), (), s32[]{:S(2)}) async-start(), calls=%async_computation.42 | async-start | bytes 327680
  736.7 438.6 %reduce-scatter.55.cloned.1.call-start = ((), (), s32[]{:S(2)}) async-start(), calls=%async_computation.39 | async-start | bytes 491520
  737.7 465.3 %reduce-scatter.63.cloned.1.call-start = ((), (), s32[]{:S(2)}) async-start(), calls=%async_computation.43 | async-start | bytes 327680
  738.7 492.0 %reduce-scatter.57.cloned.1.call-start = ((), (), s32[]{:S(2)}) async-start(), calls=%async_computation.40 | async-start | bytes 491520
  739.7 681.2 %all-reduce.11.cloned.1.call-start = ((), (), s32[]{:S(2)}) async-start(), calls=%async_computation.45 | async-start | bytes 10223616 | tf_op jit(solution)/shard_map/psum | solution.py:212
  1058.5 62.6 %copy-start.77 = (f32[1,512]{1,0:T(1,128)S(1)}, f32[1,512]{1,0:T(1,128)}, u32[]{:S(2)}) copy-start(f32[1,512]{1,0:T(1,128)} %get-tuple-element.576) | copy-start | bytes 6148
  (89 other events, 236.0 us)
Sparse Core Ops, SparseCore 0:
  9.9 39.6 all-gather.11
  52.6 27.9 all-gather.23
  82.7 27.4 all-gather.21
  112.2 36.5 all-gather.15
  150.8 35.9 all-gather.13
  238.5 21.0 all-reduce.16
  261.6 27.8 all-gather.25
  291.5 26.4 all-gather.27
  320.0 37.4 all-gather.17
  359.3 37.4 all-gather.19
  406.4 22.1 all-reduce.14
  466.7 45.0 reduce-scatter.42
  514.2 43.1 reduce-scatter.44
  559.5 59.5 reduce-scatter.30
  621.3 60.2 reduce-scatter.32
  685.8 30.3 all-reduce.12
  719.6 25.9 reduce-scatter.48
  748.5 35.1 reduce-scatter.50
  786.9 35.1 reduce-scatter.52
  825.5 28.5 reduce-scatter.36
  857.1 57.0 reduce-scatter.38
  917.2 57.0 reduce-scatter.40
  977.3 30.9 reduce-scatter.46
  1011.2 47.2 reduce-scatter.34
  1062.0 26.0 reduce-scatter.64
  1091.4 28.4 reduce-scatter.58
  1123.1 24.0 reduce-scatter.60
  1150.9 24.4 reduce-scatter.54
  1178.9 24.0 reduce-scatter.62
  1206.2 24.4 reduce-scatter.56
  1233.6 187.2 all-reduce.10
where the time goes:
time: 1450 us; the launch traced here: 1440 us
  waiting for transfers between devices  962 us (66%)
  matrix products  238 us (16%)
  blocking collectives  105 us (7%)
  local copies, waits for them, and re-layouts  70.3 us (5%)
  other arithmetic  41.6 us (3%)
  between operations  16.6 us (1%)
    psum x1, waiting for transfers between devices, run_block(): lax.psum((share_gains, share_shifts, share_head, share_qkv, share_proj, s...  168 us
    unnamed x37, waiting for transfers between devices  164 us
    reduce_scatter x2, waiting for transfers between devices, run_block(): lax.psum_scatter(grad_down, 'fsdp', scatter_dimension=1, tiled=True)  98.6 us
    reduce_scatter x2, waiting for transfers between devices, run_block(): lax.psum_scatter(grad_up, 'fsdp', scatter_dimension=0, tiled=True)  98.2 us
    reduce_scatter x2, waiting for transfers between devices, run_block(): lax.psum_scatter(grad_qkv, 'fsdp', scatter_dimension=1, tiled=True)  84.1 us
    reduce_scatter x2, waiting for transfers between devices, run_block(): lax.psum_scatter(from_heads(value_parts), 'ctx', scatter_dimension=0, til...  60.4 us
    all_gather x2, waiting for transfers between devices, run_block(): lax.all_gather(up_weight, 'fsdp', axis=0, tiled=True)  60.4 us
    all_gather x2, waiting for transfers between devices, run_block(): lax.all_gather(down_weight, 'fsdp', axis=1, tiled=True)  59.1 us
  transfers between devices with their start and end apart: 31, of which 26 were waited for; matrix products, arithmetic and copies ran while one was open for 16% of the time, Pallas kernels for 0%

commit v1 on v0

--- a/solution.py
+++ b/solution.py
@@ -4,6 +4,28 @@
 from jax.sharding import PartitionSpec as P
 
 HD = 64
+
+
+def joined_along(blocks, dim):
+    lengths = list(blocks.shape[1:])
+    lengths[dim] *= blocks.shape[0]
+    return jnp.moveaxis(blocks, 0, dim).reshape(lengths)
+
+
+def gather_around(value, axis, dim):
+    size = lax.axis_size(axis)
+    pairs = [(i, (i + 1) % size) for i in range(size)]
+    back = [(b, a) for a, b in pairs]
+    lower, upper = ([], [])
+    for step in range(size - 1):
+        if step % 2 == 0:
+            lower.append(lax.ppermute(lower[-1] if lower else value, axis, pairs))
+        else:
+            upper.append(lax.ppermute(upper[-1] if upper else value, axis, back))
+    blocks = jnp.stack([*lower[::-1], value, *upper])
+    shift = lax.axis_index(axis) - len(lower)
+    blocks = blocks[(jnp.arange(size) - shift) % size]
+    return joined_along(blocks, dim)
 
 
 def layer_stats(rows):
@@ -46,7 +68,7 @@
         lax.all_gather(qkv_weight, "fsdp", axis=1, tiled=True),
         lax.all_gather(proj_weight, "fsdp", axis=1, tiled=True),
         lax.all_gather(up_weight, "fsdp", axis=0, tiled=True),
-        lax.all_gather(down_weight, "fsdp", axis=1, tiled=True),
+        gather_around(down_weight, "fsdp", 1),
     )
     gain_vals = gain_full.astype(jnp.float32)
     shift_vals = shift_full.astype(jnp.float32)

time: 1450 us -> 1390 us (0.959)
  waiting for transfers between devices: 962 us -> 894 us
    all_gather x2 -> x0, waiting for transfers between devices: 59.1 us -> none  [run_block(): lax.all_gather(down_weight, 'fsdp', axis=1, tiled=True)]
    ppermute x0 -> x6, waiting for transfers between devices: none -> 58.4 us  [the longest x2 38.5 us: gather_around(): upper.append(lax.ppermute(upper[-1] if upper else value, axis, back))]
    all_gather x2, waiting for transfers between devices: 60.4 us -> 13.5 us  [run_block(): lax.all_gather(up_weight, 'fsdp', axis=0, tiled=True)]
    psum x3, waiting for transfers between devices: 40.2 us -> 22.1 us  [tensor_sum(): return lax.psum(partial_rows, 'tp')]
    unnamed x37 -> x35, waiting for transfers between devices: 164 us -> 162 us
    unnamed x203 -> x215, local copies, waits for them, and re-layouts: 43.6 us -> 42.3 us
  transfers between devices with their start and end apart: 31 -> 35, of which waited for: 26 -> 26; matrix products, arithmetic and copies ran while one was open for 16% -> 16% of each run, Pallas kernels for 0% -> 0%
where the time goes in v1:
time: 1390 us; the launch traced here: 1380 us
  waiting for transfers between devices  894 us (64%)
  matrix products  232 us (17%)
  blocking collectives  105 us (8%)
  local copies, waits for them, and re-layouts  75.9 us (5%)
  other arithmetic  45.1 us (3%)
  between operations  16.4 us (1%)
    psum x1, waiting for transfers between devices, run_block(): lax.psum((share_gains, share_shifts, share_head, share_qkv, share_proj, s...  168 us
    unnamed x35, waiting for transfers between devices  162 us
    reduce_scatter x2, waiting for transfers between devices, run_block(): lax.psum_scatter(grad_down, 'fsdp', scatter_dimension=1, tiled=True)  98.3 us
    reduce_scatter x2, waiting for transfers between devices, run_block(): lax.psum_scatter(grad_up, 'fsdp', scatter_dimension=0, tiled=True)  98.2 us
    reduce_scatter x2, waiting for transfers between devices, run_block(): lax.psum_scatter(grad_qkv, 'fsdp', scatter_dimension=1, tiled=True)  84.3 us
    reduce_scatter x2, waiting for transfers between devices, run_block(): lax.psum_scatter(from_heads(value_parts), 'ctx', scatter_dimension=0, til...  60.4 us
    reduce_scatter x2, waiting for transfers between devices, run_block(): lax.psum_scatter(from_heads(key_parts), 'ctx', scatter_dimension=0, tiled...  59 us
    unnamed x215, local copies, waits for them, and re-layouts  42.3 us
  transfers between devices with their start and end apart: 35, of which 26 were waited for; matrix products, arithmetic and copies ran while one was open for 16% of the time, Pallas kernels for 0%

profile of v1, /device:TPU:0, one launch (start us, length us, event | category | flops | bytes accessed | tf_op | source)
XLA Modules:
  0.0 1379.9 jit_solution(3189334577939901383)
XLA Ops:
  8.0 9.5 all_gather.56
  17.5 7.9 all_gather.59
  25.4 7.2 all_gather.57
  33.9 16.2 %all_gather.58 = bf16[3,512,256]{2,1,0:T(8,128)(2,1)S(1)} all-gather(bf16[3,128,256]{2,1,0:T(8,128)(2,1)} %param.44), channel_id=1, replica_groups=mesh['fsdp'=4,'ctx'=4,'tp'=2] {'fsdp'}, dimensions={1}, use_global_device_ids=true | all-gather | bytes 983040 | tf_op jit(solution)/shard_map/all_gather | solution.py:68
  53.6 7.6 all-gather.1
  61.4 7.5 all-gather
  70.5 9.3 all-reduce
  85.0 8.5 all_gather.62
  93.6 9.8 all_gather.54
  116.6 31.1 %while.58 = (s32[]{:T(128)}, bf16[4,512,64]{1,2,0:T(8,128)(2,1)S(1)}, f32[4,512]{1,0:T(4,128)S(1)}, bf16[4,512,64]{2,1,0:T(8,128)(2,1)}, bf16[4,2048,64]{2,1,0:T...) while((s32[]{:T(128)}, ...), condition=%wide.region_49.50_spmd.clone, body=%wide.region_46.49_spmd.clone.sunk | while | flops 280002048 | bytes 30640268 | solution.py:127
  153.9 4.2 copy.108
  158.1 28.8 %all-gather.12.cloned.1.call-done = bf16[2048,384]{1,0:T(8,128)(2,1)} async-done(((bf16[512,384]{1,0:T(8,128)(2,1)}), bf16[2048,384]{1,0:T(8,128)(2,1)}) %all-gather.12.cloned.1.call-update) | async-done | bytes 1572880 | tf_op jit(solution)/shard_map/all_gather | solution.py:109
  189.4 4.2 copy.107
  193.6 43.7 %while.56 = (s32[]{:T(128)}, bf16[6,512,64]{1,2,0:T(8,128)(2,1)S(1)}, f32[6,512]{1,0:T(8,128)S(1)}, bf16[6,512,64]{2,1,0:T(8,128)(2,1)S(1)}, bf16[6,2048,64]{2,1...) while((s32[]{:T(128)}, ...), condition=%wide.region_5.6_spmd.clone, body=%wide.region_2.5_spmd.clone.sunk | while | flops 277904896 | bytes 30638212 | solution.py:127
  244.4 13.0 collective-permute-done
  263.8 38.5 %collective-permute-done.5 = bf16[1024,128]{1,0:T(8,128)(2,1)S(1)} collective-permute-done((bf16[1024,128]{1,0:T(8,128)(2,1)S(1)}, bf16[1024,128]{1,0:T(8,128)(2,1)S(1)}, u32[]{:S(2)}, u32[]{:S(2)}) %collective-permute-start.5) | collective-permute-done | bytes 262176 | tf_op jit(solution)/shard_map/ppermute | solution.py:24
  302.3 4.3 collective-permute-done.4
  308.8 3.4 pad_maximum_fusion.1
  312.3 3.8 gather_fusion
  324.8 13.4 all-gather.16.cloned.1.call-done
  349.8 22.1 %all-reduce.15.cloned.1.call-done = (f32[512,768]{1,0:T(8,128)}, f32[512,512]{1,0:T(8,128)}) async-done(((f32[512,768]{1,0:T(8,128)}, f32[512,512]{1,0:T(8,128)}), (f32[512,768]{1,0:T(8,128)}, f32[512,512]{1,0:T(8,128)})) %all-reduce.15.cloned.1.call-update) | async-done | bytes 2621456 | tf_op jit(solution)/shard_map/psum | solution.py:48
  378.6 31.1 %while.59 = (s32[]{:T(128)}, bf16[4,512,64]{1,2,0:T(8,128)(2,1)S(1)}, f32[4,2048,64]{1,2,0:T(8,128)}, f32[4,2048,64]{1,2,0:T(8,128)}, bf16[4,512,64]{2,1,0:T(8,1...) while((s32[]{:T(128)}, ...), condition=%wide.region_59.60_spmd.clone, body=%wide.region_57.59_spmd.clone.sunk | while | flops 683834880 | bytes 40004792 | solution.py:186
  418.0 65.1 %while.57 = (s32[]{:T(128)}, bf16[6,512,64]{1,2,0:T(8,128)(2,1)}, f32[6,2048,64]{1,2,0:T(8,128)}, f32[6,2048,64]{1,2,0:T(8,128)}, bf16[6,512,64]{2,1,0:T(8,128)(...) while((s32[]{:T(128)}, bf16[6,512,64]{1,2,0:T(8,128)(2,1)}, ...), condition=%wide.region_15.16_spmd.clone, body=%wide.region_13.15_spmd.clone.sunk | while | flops 681737728 | bytes 34759800 | solution.py:186
  484.3 3.4 fusion.194
  487.8 4.9 fusion.175
  503.3 59.0 %reduce-scatter.31.cloned.1.call-done = f32[512,384]{0,1:T(8,128)} async-done(((f32[2048,384]{0,1:T(8,128)}), f32[512,384]{0,1:T(8,128)}) %reduce-scatter.31.cloned.1.call-update) | async-done | bytes 786448 | tf_op jit(solution)/shard_map/reduce_scatter | solution.py:190
  565.4 59.5 %reduce-scatter.33.cloned.1.call-done = f32[512,384]{0,1:T(8,128)} async-done(((f32[2048,384]{0,1:T(8,128)}), f32[512,384]{0,1:T(8,128)}) %reduce-scatter.33.cloned.1.call-update) | async-done | bytes 786448 | tf_op jit(solution)/shard_map/reduce_scatter | solution.py:191
  625.0 4.1 add_add_fusion
  632.4 3.4 fusion.172
  636.9 3.6 fusion.146
  643.8 5.2 fusion.174
  650.2 6.1 fusion.141
  683.3 5.8 reduce-scatter.49.cloned.1.call-done
  689.1 38.1 %reduce-scatter.51.cloned.1.call-done = f32[128,1024]{1,0:T(8,128)} async-done(((f32[512,1024]{1,0:T(8,128)}), f32[128,1024]{1,0:T(8,128)}) %reduce-scatter.51.cloned.1.call-update) | async-done | bytes 524304 | tf_op jit(solution)/shard_map/reduce_scatter | solution.py:231
  727.1 38.3 %reduce-scatter.53.cloned.1.call-done = f32[1024,128]{1,0:T(8,128)} async-done(((f32[1024,512]{1,0:T(8,128)}), f32[1024,128]{1,0:T(8,128)}) %reduce-scatter.53.cloned.1.call-update) | async-done | bytes 524304 | tf_op jit(solution)/shard_map/reduce_scatter | solution.py:232
  765.4 31.9 %reduce-scatter.37.cloned.1.call-done = f32[384,192]{0,1:T(8,128)} async-done(((f32[384,768]{0,1:T(8,128)}), f32[384,192]{0,1:T(8,128)}) %reduce-scatter.37.cloned.1.call-update) | async-done | bytes 294928 | tf_op jit(solution)/shard_map/reduce_scatter | solution.py:230
  797.3 60.1 %reduce-scatter.39.cloned.1.call-done = f32[192,1536]{1,0:T(8,128)} async-done(((f32[768,1536]{1,0:T(8,128)}), f32[192,1536]{1,0:T(8,128)}) %reduce-scatter.39.cloned.1.call-update) | async-done | bytes 1179664 | tf_op jit(solution)/shard_map/reduce_scatter | solution.py:231
  857.5 60.0 %reduce-scatter.41.cloned.1.call-done = f32[1536,192]{0,1:T(8,128)} async-done(((f32[1536,768]{0,1:T(8,128)}), f32[1536,192]{0,1:T(8,128)}) %reduce-scatter.41.cloned.1.call-update) | async-done | bytes 1179664 | tf_op jit(solution)/shard_map/reduce_scatter | solution.py:232
  917.4 33.9 %reduce-scatter.47.cloned.1.call-done = f32[3,128,256]{2,1,0:T(8,128)} async-done(((f32[3,512,256]{2,1,0:T(8,128)}), f32[3,128,256]{2,1,0:T(8,128)}) %reduce-scatter.47.cloned.1.call-update) | async-done | bytes 393232 | tf_op jit(solution)/shard_map/reduce_scatter | solution.py:229
  951.4 50.3 %reduce-scatter.35.cloned.1.call-done = f32[3,192,384]{2,1,0:T(8,128)} async-done(((f32[3,768,384]{2,1,0:T(8,128)}), f32[3,192,384]{2,1,0:T(8,128)}) %reduce-scatter.35.cloned.1.call-update) | async-done | bytes 884752 | tf_op jit(solution)/shard_map/reduce_scatter | solution.py:229
  1001.7 29.6 %reduce-scatter.65.cloned.1.call-done = f32[384,1]{1,0:T(8,128)} async-done(((f32[1536,1]{1,0:T(8,128)}), f32[384,1]{1,0:T(8,128)}) %reduce-scatter.65.cloned.1.call-update) | async-done | bytes 1552
  1032.3 30.9 %reduce-scatter.59.cloned.1.call-done = f32[576,1]{1,0:T(8,128)} async-done(((f32[2304,1]{1,0:T(8,128)}), f32[576,1]{1,0:T(8,128)}) %reduce-scatter.59.cloned.1.call-update) | async-done | bytes 2320
  1072.1 18.6 %reduce-scatter.61.cloned.1.call-done = f32[128,2]{1,0:T(8,128)} async-done(((f32[512,2]{1,0:T(8,128)}), f32[128,2]{1,0:T(8,128)}) %reduce-scatter.61.cloned.1.call-update) | async-done | bytes 1040
  1091.6 27.0 %reduce-scatter.55.cloned.1.call-done = f32[192,2]{1,0:T(8,128)} async-done(((f32[768,2]{1,0:T(8,128)}), f32[192,2]{1,0:T(8,128)}) %reduce-scatter.55.cloned.1.call-update) | async-done | bytes 1552
  1119.5 26.5 %reduce-scatter.63.cloned.1.call-done = f32[128,4]{1,0:T(8,128)} async-done(((f32[512,4]{1,0:T(8,128)}), f32[128,4]{1,0:T(8,128)}) %reduce-scatter.63.cloned.1.call-update) | async-done | bytes 2064
  1147.0 26.9 %reduce-scatter.57.cloned.1.call-done = f32[192,4]{1,0:T(8,128)} async-done(((f32[768,4]{1,0:T(8,128)}), f32[192,4]{1,0:T(8,128)}) %reduce-scatter.57.cloned.1.call-update) | async-done | bytes 3088
  1174.8 21.5 %all-reduce.1 = (f32[2,192]{1,0:T(2,128)}, f32[4,192]{1,0:T(4,128)}, f32[1,576]{1,0:T(1,128)}, f32[2,128]{1,0:T(2,128)}, f32[4,128]{1,0:T(4,128)}, /*index=5*/f32[1,384]{1,0:T(1,128)}) all-reduce(f32[2,192]{1,0:T(2,128)S(1)} %copy.122, f32[4,192]{1,0:T(4,128)S(1)} %copy.124, ...), channel_id=1, replica_groups=mesh['fsdp'=4,'ctx'=4,'tp'=2] {'ctx'}, use_global_device_ids=true, to_apply=%region_24.25 | all-reduce | flops 2880 | bytes 23040 | tf_op jit(solution)/shard_map/psum | solution.py:234
  1196.3 167.8 %all-reduce.11.cloned.1.call-done = (f32[3,192,384]{2,1,0:T(8,128)}, f32[384,192]{0,1:T(8,128)}, f32[192,1536]{1,0:T(8,128)}, f32[1536,192]{0,1:T(8,128)}, f32[3...) async-done(((f32[3,192,384]{2,1,0:T(8,128)}, f32[384,192]{0,1:T(8,128)}, f32[192,1536]{1,0:T(8,128)}, f32[1536,192]{0,1:T(8,128)}, ...) | async-done | bytes 5111824 | tf_op jit(solution)/shard_map/psum | solution.py:234
  (567 shorter events, 327.0 us)
Async XLA Ops:
  7.2 42.9 %copy-start.6 = (bf16[1,512,512]{2,1,0:T(8,128)(2,1)S(1)}, bf16[1,512,512]{2,1,0:T(8,128)(2,1)}, u32[]{:S(2)}) copy-start(bf16[1,512,512]{2,1,0:T(8,128)(2,1)} %param.38) | copy-start | bytes 1572868
  7.2 73.8 %all-gather.10.cloned.1.call-start = ((), (), s32[]{:S(2)}) async-start(), calls=%async_computation.18 | async-start | bytes 2211840 | tf_op jit(solution)/shard_map/all_gather | solution.py:68
  7.9 95.5 %all-gather.20.cloned.1.call-start = ((), (), s32[]{:S(2)}) async-start(), calls=%async_computation.29 | async-start | bytes 1310720 | tf_op jit(solution)/shard_map/all_gather | solution.py:110
  50.1 33.6 %copy-start.23 = (bf16[3,512,256]{2,1,0:T(8,128)(2,1)}, bf16[3,512,256]{2,1,0:T(8,128)(2,1)S(1)}, u32[]{:S(2)}) copy-start(bf16[3,512,256]{2,1,0:T(8,128)(2,1)S(1)} %all_gather.58) | copy-start | bytes 2359300
  50.5 29.9 %copy-start.4 = (bf16[1,512,768]{2,1,0:T(8,128)(2,1)S(1)}, bf16[1,512,768]{2,1,0:T(8,128)(2,1)}, u32[]{:S(2)}) copy-start(bf16[1,512,768]{2,1,0:T(8,128)(2,1)} %param.28) | copy-start | bytes 2359300
  51.4 32.3 %copy-start.33 = (bf16[512,512]{1,0:T(8,128)(2,1)}, bf16[512,512]{1,0:T(8,128)(2,1)S(1)}, u32[]{:S(2)}) copy-start(bf16[512,512]{1,0:T(8,128)(2,1)S(1)} %fusion.145) | copy-start | bytes 1572868
  52.4 57.8 %all-gather.18.cloned.1.call-start = ((), (), s32[]{:S(2)}) async-start(), calls=%async_computation.28 | async-start | bytes 1310720 | tf_op jit(solution)/shard_map/all_gather | solution.py:109
  53.5 97.8 %all-gather.14.cloned.1.call-start = ((), (), s32[]{:S(2)}) async-start(), calls=%async_computation.20 | async-start | bytes 1966080 | tf_op jit(solution)/shard_map/all_gather | solution.py:110
  79.8 69.3 %copy-start.62 = (f32[768]{0:T(1024)}, f32[768]{0:T(1024)S(1)}, u32[]{:S(2)}) copy-start(f32[768]{0:T(1024)S(1)} %get-tuple-element.493) | copy-start | bytes 9220
  80.4 68.7 %copy-start.84 = (f32[768]{0:T(1024)}, f32[768]{0:T(1024)S(1)}, u32[]{:S(2)}) copy-start(f32[768]{0:T(1024)S(1)} %get-tuple-element.489) | copy-start | bytes 9220
  80.4 257.8 %copy-start.86 = (f32[768]{0:T(1024)}, f32[768]{0:T(1024)S(1)}, u32[]{:S(2)}) copy-start(f32[768]{0:T(1024)S(1)} %get-tuple-element.487) | copy-start | bytes 9220
  80.6 68.5 %copy-start.68 = (f32[512]{0:T(512)}, f32[512]{0:T(512)S(1)}, u32[]{:S(2)}) copy-start(f32[512]{0:T(512)S(1)} %broadcast_multiply_fusion.11) | copy-start | bytes 6148
  81.0 68.1 %copy-start.70 = (f32[512]{0:T(512)}, f32[512]{0:T(512)S(1)}, u32[]{:S(2)}) copy-start(f32[512]{0:T(512)S(1)} %add_rsqrt_fusion.3) | copy-start | bytes 6148
  83.6 103.3 %all-gather.12.cloned.1.call-start = ((), (), s32[]{:S(2)}) async-start(), calls=%async_computation.19 | async-start | bytes 1966080 | tf_op jit(solution)/shard_map/all_gather | solution.py:109
  93.5 54.3 %copy-start.29 = (bf16[256,512]{1,0:T(8,128)(2,1)}, bf16[256,512]{1,0:T(8,128)(2,1)S(1)}, u32[]{:S(2)}) copy-start(bf16[256,512]{1,0:T(8,128)(2,1)S(1)} %all_gather.62) | copy-start | bytes 786436
  103.4 134.0 %copy-start.16 = (bf16[384,768]{0,1:T(8,128)(2,1)}, bf16[384,768]{0,1:T(8,128)(2,1)S(1)}, u32[]{:S(2)}) copy-start(bf16[384,768]{0,1:T(8,128)(2,1)S(1)} %all_gather.54) | copy-start | bytes 1769476
  116.1 200.0 %all-reduce.17.cloned.1.call-start = ((), (), s32[]{:S(2)}) async-start(), calls=%async_computation.46 | async-start | bytes 5242880 | tf_op jit(solution)/shard_map/psum | solution.py:48
  239.1 67.5 %copy-start.55 = (bf16[1024,128]{1,0:T(8,128)(2,1)S(1)}, bf16[1024,128]{1,0:T(8,128)(2,1)}, u32[]{:S(2)}) copy-start(bf16[1024,128]{1,0:T(8,128)(2,1)} %param.47) | copy-start | bytes 786436
  239.2 79.4 %all-gather.22.cloned.1.call-start = ((), (), s32[]{:S(2)}) async-start(), calls=%async_computation.30 | async-start | bytes 1310720 | tf_op jit(solution)/shard_map/all_gather | solution.py:70
  239.9 98.3 %all-gather.16.cloned.1.call-start = ((), (), s32[]{:S(2)}) async-start(), calls=%async_computation.21 | async-start | bytes 2949120 | tf_op jit(solution)/shard_map/all_gather | solution.py:70
  240.0 17.5 %collective-permute-start = (bf16[1536,192]{0,1:T(8,128)(2,1)}, bf16[1536,192]{0,1:T(8,128)(2,1)}, u32[]{:S(2)}, u32[]{:S(2)}) collective-permute-start(bf16[1536,192]{0,1:T(8,128)(2,1)} %param.37), channel_id=1, source_target_pairs={{0,8},{8,16},{16,24},{24,0},{1,9},{9,17},{17,25},{25,1},{2,10},{10... | collective-permute-start | bytes 1769480 | tf_op jit(solution)/shard_map/ppermute | solution.py:22
  241.5 21.5 %collective-permute-start.3 = (bf16[1024,128]{1,0:T(8,128)(2,1)S(1)}, bf16[1024,128]{1,0:T(8,128)(2,1)S(1)}, u32[]{:S(2)}, u32[]{:S(2)}) collective-permute-start(bf16[1024,128]{1,0:T(8,128)(2,1)S(1)} %copy-done.54), channel_id=1, source_target_pairs={{0,8},{8,16},{16,24},{24,0},{1,9},{9,17},{17,25},{25,1},{2,10},{10... | collective-permute-start | bytes 786440 | tf_op jit(solution)/shard_map/ppermute | solution.py:22
  242.9 65.9 %collective-permute-start.2 = (bf16[1536,192]{0,1:T(8,128)(2,1)}, bf16[1536,192]{0,1:T(8,128)(2,1)}, u32[]{:S(2)}, u32[]{:S(2)}) collective-permute-start(bf16[1536,192]{0,1:T(8,128)(2,1)} %param.37), channel_id=1, source_target_pairs={{8,0},{16,8},{24,16},{0,24},{9,1},{17,9},{25,17},{1,25},{10,2},{18... | collective-permute-start | bytes 1769480 | tf_op jit(solution)/shard_map/ppermute | solution.py:24
  257.5 51.4 %collective-permute-start.1 = (bf16[1536,192]{0,1:T(8,128)(2,1)}, bf16[1536,192]{0,1:T(8,128)(2,1)}, u32[]{:S(2)}, u32[]{:S(2)}) collective-permute-start(bf16[1536,192]{0,1:T(8,128)(2,1)} %collective-permute-done), channel_id=1, source_target_pairs={{0,8},{8,16},{16,24},{24,0},{1,9},{9,17},{17,25},{25,1},{2,10},{10... | collective-permute-start | bytes 1769480 | tf_op jit(solution)/shard_map/ppermute | solution.py:22
  258.0 44.3 %collective-permute-start.5 = (bf16[1024,128]{1,0:T(8,128)(2,1)S(1)}, bf16[1024,128]{1,0:T(8,128)(2,1)S(1)}, u32[]{:S(2)}, u32[]{:S(2)}) collective-permute-start(bf16[1024,128]{1,0:T(8,128)(2,1)S(1)} %copy-done.54), channel_id=1, source_target_pairs={{8,0},{16,8},{24,16},{0,24},{9,1},{17,9},{25,17},{1,25},{10,2},{18... | collective-permute-start | bytes 786440 | tf_op jit(solution)/shard_map/ppermute | solution.py:24
  260.4 111.5 %all-reduce.15.cloned.1.call-start = ((), (), s32[]{:S(2)}) async-start(), calls=%async_computation.45 | async-start | bytes 5242880 | tf_op jit(solution)/shard_map/psum | solution.py:48
  263.0 43.7 %collective-permute-start.4 = (bf16[1024,128]{1,0:T(8,128)(2,1)S(1)}, bf16[1024,128]{1,0:T(8,128)(2,1)S(1)}, u32[]{:S(2)}, u32[]{:S(2)}) collective-permute-start(bf16[1024,128]{1,0:T(8,128)(2,1)S(1)} %collective-permute-done.3), channel_id=1, source_target_pairs={{0,8},{8,16},{16,24},{24,0},{1,9},{9,17},{17,25},{25,1},{2,10},{10... | collective-permute-start | bytes 786440 | tf_op jit(solution)/shard_map/ppermute | solution.py:22
  349.5 147.5 %reduce-scatter.43.cloned.1.call-start = ((), (), s32[]{:S(2)}) async-start(), calls=%async_computation.31 | async-start | bytes 2621440 | tf_op jit(solution)/shard_map/reduce_scatter | solution.py:190
  409.8 90.8 %reduce-scatter.45.cloned.1.call-start = ((), (), s32[]{:S(2)}) async-start(), calls=%async_computation.32 | async-start | bytes 2621440 | tf_op jit(solution)/shard_map/reduce_scatter | solution.py:191
  418.0 144.4 %reduce-scatter.31.cloned.1.call-start = ((), (), s32[]{:S(2)}) async-start(), calls=%async_computation.22 | async-start | bytes 3932160 | tf_op jit(solution)/shard_map/reduce_scatter | solution.py:190
  483.1 141.9 %reduce-scatter.33.cloned.1.call-start = ((), (), s32[]{:S(2)}) async-start(), calls=%async_computation.23 | async-start | bytes 3932160 | tf_op jit(solution)/shard_map/reduce_scatter | solution.py:191
  483.9 192.4 %all-reduce.13.cloned.1.call-start = ((), (), s32[]{:S(2)}) async-start(), calls=%async_computation.44 | async-start | bytes 10485760 | tf_op jit(solution)/shard_map/psum | solution.py:48
  629.1 60.0 %reduce-scatter.49.cloned.1.call-start = ((), (), s32[]{:S(2)}) async-start(), calls=%async_computation.34 | async-start | bytes 655360 | tf_op jit(solution)/shard_map/reduce_scatter | solution.py:230
  632.3 94.8 %reduce-scatter.51.cloned.1.call-start = ((), (), s32[]{:S(2)}) async-start(), calls=%async_computation.35 | async-start | bytes 2621440 | tf_op jit(solution)/shard_map/reduce_scatter | solution.py:231
  635.9 129.6 %reduce-scatter.53.cloned.1.call-start = ((), (), s32[]{:S(2)}) async-start(), calls=%async_computation.36 | async-start | bytes 2621440 | tf_op jit(solution)/shard_map/reduce_scatter | solution.py:232
  640.5 156.9 %reduce-scatter.37.cloned.1.call-start = ((), (), s32[]{:S(2)}) async-start(), calls=%async_computation.25 | async-start | bytes 1474560 | tf_op jit(solution)/shard_map/reduce_scatter | solution.py:230
  643.7 213.7 %reduce-scatter.39.cloned.1.call-start = ((), (), s32[]{:S(2)}) async-start(), calls=%async_computation.26 | async-start | bytes 5898240 | tf_op jit(solution)/shard_map/reduce_scatter | solution.py:231
  649.0 268.4 %reduce-scatter.41.cloned.1.call-start = ((), (), s32[]{:S(2)}) async-start(), calls=%async_computation.27 | async-start | bytes 5898240 | tf_op jit(solution)/shard_map/reduce_scatter | solution.py:232
  656.4 294.9 %reduce-scatter.47.cloned.1.call-start = ((), (), s32[]{:S(2)}) async-start(), calls=%async_computation.33 | async-start | bytes 1966080 | tf_op jit(solution)/shard_map/reduce_scatter | solution.py:229
  662.4 339.3 %reduce-scatter.35.cloned.1.call-start = ((), (), s32[]{:S(2)}) async-start(), calls=%async_computation.24 | async-start | bytes 4423680 | tf_op jit(solution)/shard_map/reduce_scatter | solution.py:229
  668.6 362.7 %reduce-scatter.65.cloned.1.call-start = ((), (), s32[]{:S(2)}) async-start(), calls=%async_computation.42 | async-start | bytes 983040
  673.4 389.8 %reduce-scatter.59.cloned.1.call-start = ((), (), s32[]{:S(2)}) async-start(), calls=%async_computation.39 | async-start | bytes 1474560
  676.2 414.4 %reduce-scatter.61.cloned.1.call-start = ((), (), s32[]{:S(2)}) async-start(), calls=%async_computation.40 | async-start | bytes 327680
  680.1 438.4 %reduce-scatter.55.cloned.1.call-start = ((), (), s32[]{:S(2)}) async-start(), calls=%async_computation.37 | async-start | bytes 491520
  681.2 464.9 %reduce-scatter.63.cloned.1.call-start = ((), (), s32[]{:S(2)}) async-start(), calls=%async_computation.41 | async-start | bytes 327680
  682.2 491.7 %reduce-scatter.57.cloned.1.call-start = ((), (), s32[]{:S(2)}) async-start(), calls=%async_computation.38 | async-start | bytes 491520
  683.2 680.9 %all-reduce.11.cloned.1.call-start = ((), (), s32[]{:S(2)}) async-start(), calls=%async_computation.43 | async-start | bytes 10223616 | tf_op jit(solution)/shard_map/psum | solution.py:234
  1001.7 62.7 %copy-start.83 = (f32[1,512]{1,0:T(1,128)S(1)}, f32[1,512]{1,0:T(1,128)}, u32[]{:S(2)}) copy-start(f32[1,512]{1,0:T(1,128)} %get-tuple-element.616) | copy-start | bytes 6148
  (99 other events, 331.2 us)
Sparse Core Ops, SparseCore 0:
  9.9 39.6 all-gather.9
  52.6 27.9 all-gather.19
  82.7 27.4 all-gather.17
  112.2 36.5 all-gather.13
  150.8 35.9 all-gather.11
  239.3 21.0 all-reduce.16
  262.4 36.3 all-gather.21
  300.7 37.4 all-gather.15
  349.6 22.2 all-reduce.14
  409.9 45.0 reduce-scatter.42
  457.3 43.1 reduce-scatter.44
  502.7 59.5 reduce-scatter.30
  564.7 60.2 reduce-scatter.32
  629.2 30.3 all-reduce.12
  663.1 25.9 reduce-scatter.48
  691.9 35.1 reduce-scatter.50
  730.2 35.1 reduce-scatter.52
  768.8 28.5 reduce-scatter.36
  800.3 57.0 reduce-scatter.38
  860.3 57.0 reduce-scatter.40
  920.4 30.8 reduce-scatter.46
  954.4 47.2 reduce-scatter.34
  1005.2 26.0 reduce-scatter.64
  1034.6 28.5 reduce-scatter.58
  1066.5 24.0 reduce-scatter.60
  1094.1 24.4 reduce-scatter.54
  1122.0 24.0 reduce-scatter.62
  1149.4 24.4 reduce-scatter.56
  1176.8 187.2 all-reduce.10
